TPU v7x, 512 devices: a whole 4x8x8 slice. The times are simulated.
512 devices in a mesh: grp: 32 (over y_hi, x, core), row: 16 (over y_lo, z).
Axes of the slice: x: 4, y: 8 (y_hi: 4, y_lo: 2; y = y_hi * 2 + y_lo), z: 8, core: 2. Of those that a mesh axis runs over, the one named last changes fastest.
Arguments:
- starter: float32 [2, 256, 256, 512], P(None, 'grp', 'row'), may hold values from -6 to 6
- medium: float32 [256, 512], P('row'), may hold values from -0.5 to 0.5
- csm: float32 [2, 256, 256], replicated, as said below
- capon_weight: float32 [2, 256, 256], replicated, as said below
- search_cells: int32 [16, 8192], P('row'), may hold values from 0 to 8191, each once within a row
Outputs:
- bartlett_power: float32 [16, 8192], P('row', 'grp')
- capon_power: float32 [16, 8192], P('row', 'grp')
Inputs may be any that keep to these rules, and one draw needn't show every extreme that they name: `search_cells`: each row is a permutation of the 8192 cells of its slab. csm[0] + i csm[1] is Hermitian and positive definite. capon_weight[0] + i capon_weight[1] is Hermitian and positive definite.
All inputs are finite; a program needn't handle non-finite values.
Results may differ from a plain program's by a relative error of at most 0.00005.
Values sent between devices are 32-bit elements; how exact they have to be, the bound alone decides.
A program may use at most 64 MiB of HBM per device.

v0:
```python
import jax
import jax.numpy as jnp
from jax import lax
from jax.sharding import PartitionSpec as P

STEPS = 2


lap_scale = 0.5
first_coef = (0.0, 0.25)
second_coef = (-0.03, -0.02)


def padded(cells, sides, width):
    for axis, dim in sides:
        count = lax.axis_size(axis)
        ends = count - 1
        head = lax.slice_in_dim(cells, 0, width, axis=dim)
        tail = lax.slice_in_dim(cells, cells.shape[dim] - width, cells.shape[dim], axis=dim)
        cells = jnp.concatenate(
            [
                lax.ppermute(tail, axis, [(i, (i + 1) % count) for i in range(ends)]),
                cells,
                lax.ppermute(head, axis, [((i + 1) % count, i) for i in range(ends)]),
            ],
            axis=dim,
        )
    return cells


def combine(coef, values):
    real_part = coef[0] * values[0] - coef[1] * values[1]
    imag_part = coef[1] * values[0] + coef[0] * values[1]
    return jnp.stack([real_part, imag_part], axis=0)


def apply_operator(extended, medium):
    center = extended[:, :, 1:-1]
    cross_padded = jnp.pad(center, ((0, 0), (0, 0), (0, 0), (1, 1)))
    laplace = (
        extended[:, :, 2:]
        + extended[:, :, :-2]
        + cross_padded[..., 2:]
        + cross_padded[..., :-2]
        - 4.0 * center
    )
    return lap_scale * laplace + medium * center


def with_rim(field):
    return padded(field, (("row", 2),), 1)


def real_form(matrix):
    real_part = matrix[0]
    imag_part = matrix[1]
    return jnp.concatenate(
        [
            jnp.concatenate([real_part, -imag_part], axis=1),
            jnp.concatenate([imag_part, real_part], axis=1),
        ],
        axis=0,
    )


def on_device(starter, medium, csm, capon_weight, search_cells):
    slab_rows = starter.shape[2]
    cross_cells = starter.shape[3]
    hydro_dev = starter.shape[1]
    field = starter
    for marching in range(STEPS):
        first_pass = apply_operator(with_rim(field), medium)
        second_pass = apply_operator(with_rim(first_pass), medium)
        field = field + combine(first_coef, first_pass) + combine(second_coef, second_pass)
    owners = lax.axis_size("grp")
    cell_table = field.reshape(2 * hydro_dev, slab_rows * cross_cells).T
    picked = jnp.take(cell_table, search_cells[0], axis=0).reshape(owners, -1, 2, hydro_dev)
    embed_t = real_form(csm).T
    weighting_t = real_form(capon_weight).T
    gathered = lax.all_to_all(picked, "grp", split_axis=0, concat_axis=3, tiled=True)
    vectors = gathered.reshape(gathered.shape[1], 2 * gathered.shape[3])
    power = jnp.sum(vectors * vectors, axis=1) + 1e-06
    bartlett = (
        jnp.sum(vectors * jnp.dot(vectors, embed_t, precision=lax.Precision.HIGHEST), axis=1)
        / power
    )
    capon = power / jnp.sum(
        vectors * jnp.dot(vectors, weighting_t, precision=lax.Precision.HIGHEST), axis=1
    )
    result = jnp.stack([bartlett, capon], axis=0)
    return (result[0][None, :], result[1][None, :])


def solution(mesh):
    return jax.shard_map(
        on_device,
        mesh=mesh,
        in_specs=(P(None, "grp", "row", None), P("row", None), P(), P(), P("row", None)),
        out_specs=(P("row", "grp"), P("row", "grp")),
        check_vma=False,
    )
```

profile of v0, /device:TPU:9, one launch (start us, length us, event | category | flops | bytes accessed | tf_op | source)
XLA Modules:
  0.0 124.7 jit_solution(9406768473061579342)
XLA Ops:
  0.6 0.0 copy-start
  0.6 0.0 copy-start.3
  0.7 1.1 fusion.51
  1.8 10.6 %collective-permute-start = (f32[2,8,1,512]{3,2,1,0:T(1,128)S(1)}, f32[2,8,1,512]{3,2,1,0:T(1,128)S(1)}, u32[]{:S(2)}, u32[]{:S(2)}) collective-permute-start(f32[2,8,1,512]{3,2,1,0:T(1,128)S(1)} %get-tuple-element.20), channel_id=1, source_target_pairs={{1,0},{2,1},{3,2},{4,3},{5,4},{6,5},{7,6},{8,7},{9,8},{10,9},{11,1... | collective-permute-start | bytes 98312 | tf_op jit(solution)/shard_map/ppermute | solution.py:24
  12.4 1.9 %collective-permute-start.1 = (f32[2,8,1,512]{3,2,1,0:T(1,128)S(1)}, f32[2,8,1,512]{3,2,1,0:T(1,128)S(1)}, u32[]{:S(2)}, u32[]{:S(2)}) collective-permute-start(f32[2,8,1,512]{3,2,1,0:T(1,128)S(1)} %get-tuple-element.21), channel_id=1, source_target_pairs={{0,1},{1,2},{2,3},{3,4},{4,5},{5,6},{6,7},{7,8},{8,9},{9,10},{10,1... | collective-permute-start | bytes 98312 | tf_op jit(solution)/shard_map/ppermute | solution.py:22
  14.3 0.8 compare_select_fusion
  15.1 0.5 broadcast.126
  15.6 1.5 %reduce.4 = s32[8192]{0:T(1024)S(1)} reduce(s32[1,8192]{1,0:T(1,128)} %param.9, s32[]{:T(128)} %broadcast.126), dimensions={0}, to_apply=%param.9.reduce_sub_computation.3 | reduce | bytes 65540 | tf_op args[4]
  17.1 0.0 collective-permute-done
  17.1 2.0 %collective-permute-done.1 = f32[2,8,1,512]{3,2,1,0:T(1,128)S(1)} collective-permute-done((f32[2,8,1,512]{3,2,1,0:T(1,128)S(1)}, f32[2,8,1,512]{3,2,1,0:T(1,128)S(1)}, u32[]{:S(2)}, u32[]{:S(2)}) %collective-permute-start.1) | collective-permute-done | bytes 32800 | tf_op jit(solution)/shard_map/ppermute | solution.py:22
  19.1 2.5 %fusion.20 = f32[2,8,16,512]{3,2,1,0:T(8,128)S(1)} fusion(f32[2,8,16,512]{3,2,1,0:T(8,128)} %param.5, f32[2,8,1,512]{3,2,1,0:T(1,128)S(1)} %collective-permute-done.1, f32[2,8,1,512]{3,2,1,0:T(1,128)S(1)} %collective-permute-done, f32[16,512]{1,0:T(8,128)} %param.6), kind=kLoop, calls=%fused_computation.31 | loop fusion | flops 1310720 | bytes 1146880 | tf_op jit(solution)/shard_map/add | solution.py:47
  21.7 0.1 fusion.50
  21.7 3.5 %collective-permute-start.2 = (f32[2,8,1,512]{3,2,1,0:T(1,128)S(1)}, f32[2,8,1,512]{3,2,1,0:T(1,128)S(1)}, u32[]{:S(2)}, u32[]{:S(2)}) collective-permute-start(f32[2,8,1,512]{3,2,1,0:T(1,128)S(1)} %get-tuple-element.16), channel_id=1, source_target_pairs={{1,0},{2,1},{3,2},{4,3},{5,4},{6,5},{7,6},{8,7},{9,8},{10,9},{11,1... | collective-permute-start | bytes 98312 | tf_op jit(solution)/shard_map/ppermute | solution.py:24
  25.2 1.9 %collective-permute-start.3 = (f32[2,8,1,512]{3,2,1,0:T(1,128)S(1)}, f32[2,8,1,512]{3,2,1,0:T(1,128)S(1)}, u32[]{:S(2)}, u32[]{:S(2)}) collective-permute-start(f32[2,8,1,512]{3,2,1,0:T(1,128)S(1)} %get-tuple-element.17), channel_id=1, source_target_pairs={{0,1},{1,2},{2,3},{3,4},{4,5},{5,6},{6,7},{7,8},{8,9},{9,10},{10,1... | collective-permute-start | bytes 98312 | tf_op jit(solution)/shard_map/ppermute | solution.py:22
  27.1 0.1 multiply_subtract_fusion.3
  27.2 0.0 collective-permute-done.2
  27.2 4.8 %collective-permute-done.3 = f32[2,8,1,512]{3,2,1,0:T(1,128)S(1)} collective-permute-done((f32[2,8,1,512]{3,2,1,0:T(1,128)S(1)}, f32[2,8,1,512]{3,2,1,0:T(1,128)S(1)}, u32[]{:S(2)}, u32[]{:S(2)}) %collective-permute-start.3) | collective-permute-done | bytes 32800 | tf_op jit(solution)/shard_map/ppermute | solution.py:22
  32.0 1.1 fusion.25
  33.1 0.1 multiply_subtract_fusion.2
  33.2 0.0 copy-done
  33.2 0.2 fusion.40
  33.4 0.1 fusion.49
  33.4 1.9 %collective-permute-start.4 = (f32[2,8,1,512]{3,2,1,0:T(1,128)S(1)}, f32[2,8,1,512]{3,2,1,0:T(1,128)S(1)}, u32[]{:S(2)}, u32[]{:S(2)}) collective-permute-start(f32[2,8,1,512]{3,2,1,0:T(1,128)S(1)} %get-tuple-element.12), channel_id=1, source_target_pairs={{1,0},{2,1},{3,2},{4,3},{5,4},{6,5},{7,6},{8,7},{9,8},{10,9},{11,1... | collective-permute-start | bytes 98312 | tf_op jit(solution)/shard_map/ppermute | solution.py:24
  35.4 3.4 %collective-permute-start.5 = (f32[2,8,1,512]{3,2,1,0:T(1,128)S(1)}, f32[2,8,1,512]{3,2,1,0:T(1,128)S(1)}, u32[]{:S(2)}, u32[]{:S(2)}) collective-permute-start(f32[2,8,1,512]{3,2,1,0:T(1,128)S(1)} %get-tuple-element.13), channel_id=1, source_target_pairs={{0,1},{1,2},{2,3},{3,4},{4,5},{5,6},{6,7},{7,8},{8,9},{9,10},{10,1... | collective-permute-start | bytes 98312 | tf_op jit(solution)/shard_map/ppermute | solution.py:22
  38.7 0.0 collective-permute-done.4
  38.8 3.4 %collective-permute-done.5 = f32[2,8,1,512]{3,2,1,0:T(1,128)S(1)} collective-permute-done((f32[2,8,1,512]{3,2,1,0:T(1,128)S(1)}, f32[2,8,1,512]{3,2,1,0:T(1,128)S(1)}, u32[]{:S(2)}, u32[]{:S(2)}) %collective-permute-start.5) | collective-permute-done | bytes 32800 | tf_op jit(solution)/shard_map/ppermute | solution.py:22
  42.1 0.0 copy-done.3
  42.1 0.5 fusion.30
  42.6 0.1 fusion.48
  42.7 1.9 %collective-permute-start.6 = (f32[2,8,1,512]{3,2,1,0:T(1,128)S(1)}, f32[2,8,1,512]{3,2,1,0:T(1,128)S(1)}, u32[]{:S(2)}, u32[]{:S(2)}) collective-permute-start(f32[2,8,1,512]{3,2,1,0:T(1,128)S(1)} %get-tuple-element.8), channel_id=1, source_target_pairs={{1,0},{2,1},{3,2},{4,3},{5,4},{6,5},{7,6},{8,7},{9,8},{10,9},{11,1... | collective-permute-start | bytes 98312 | tf_op jit(solution)/shard_map/ppermute | solution.py:24
  44.6 3.4 %collective-permute-start.7 = (f32[2,8,1,512]{3,2,1,0:T(1,128)S(1)}, f32[2,8,1,512]{3,2,1,0:T(1,128)S(1)}, u32[]{:S(2)}, u32[]{:S(2)}) collective-permute-start(f32[2,8,1,512]{3,2,1,0:T(1,128)S(1)} %get-tuple-element.9), channel_id=1, source_target_pairs={{0,1},{1,2},{2,3},{3,4},{4,5},{5,6},{6,7},{7,8},{8,9},{9,10},{10,1... | collective-permute-start | bytes 98312 | tf_op jit(solution)/shard_map/ppermute | solution.py:22
  48.0 0.1 multiply_subtract_fusion.1
  48.1 0.0 collective-permute-done.6
  48.1 3.3 %collective-permute-done.7 = f32[2,8,1,512]{3,2,1,0:T(1,128)S(1)} collective-permute-done((f32[2,8,1,512]{3,2,1,0:T(1,128)S(1)}, f32[2,8,1,512]{3,2,1,0:T(1,128)S(1)}, u32[]{:S(2)}, u32[]{:S(2)}) %collective-permute-start.7) | collective-permute-done | bytes 32800 | tf_op jit(solution)/shard_map/ppermute | solution.py:22
  51.4 0.5 fusion.35
  51.9 0.1 multiply_subtract_fusion
  52.0 0.3 fusion.42
  52.3 0.3 copy.21
  52.6 2.6 %copy.15 = f32[16,8192]{0,1:T(8,128)} copy(f32[16,8192]{1,0:T(8,128)S(1)} %bitcast.40) | data formatting | bytes 1048576 | tf_op jit(solution)/shard_map/reshape | solution.py:76
  55.2 29.9 %gather_fusion = f32[8192,16]{1,0:T(8,128)} fusion(f32[8192,16]{1,0:T(8,128)} %bitcast.38, s32[8192]{0:T(1024)S(1)} %broadcast_clamp_fusion), kind=kCustom, calls=%fused_computation | custom fusion | bytes 1081344 | tf_op jit(solution)/shard_map/jit(_take)/gather | solution.py:77
  85.1 0.0 copy-start.1
  85.1 0.0 copy-start.2
  85.1 2.9 %copy.16 = f32[8192,16]{0,1:T(8,128)S(1)} copy(f32[8192,16]{1,0:T(8,128)} %gather_fusion) | data formatting | bytes 1048576 | tf_op jit(solution)/shard_map/jit(_take)/gather | solution.py:77
  88.0 0.2 bitcast_select_fusion
  88.2 1.1 copy.17
  89.3 14.7 %all-to-all-start = ((f32[32,256,2,8]{1,3,2,0:T(8,128)}), f32[32,256,2,8]{1,3,2,0:T(8,128)S(1)}, u32[]{:S(2)}, u32[]{:S(2)}) async-start(f32[32,256,2,8]{1,3,2,0:T(8,128)} %copy.17), calls=%async_computation | async-start | bytes 1048576 | tf_op jit(solution)/shard_map/all_to_all | solution.py:80
  104.0 0.0 copy-done.1
  104.0 0.0 copy-done.2
  104.2 15.8 %all-to-all-done = f32[32,256,2,8]{1,3,2,0:T(8,128)S(1)} async-done(((f32[32,256,2,8]{1,3,2,0:T(8,128)}), f32[32,256,2,8]{1,3,2,0:T(8,128)S(1)}, u32[]{:S(2)}, u32[]{:S(2)}) %all-to-all-start) | async-done | bytes 524320 | tf_op jit(solution)/shard_map/all_to_all | solution.py:80
  120.0 0.2 copy.19
  120.2 1.9 %fusion = f32[256]{0:T(256)S(1)} fusion(f32[256,512]{1,0:T(8,128)S(1)} %copy.19, f32[256,512]{0,1:T(8,128)S(1)} %bitcast.42, f32[256,256]{1,0:T(8,128)S(1)} %get-tuple-element.5, f32[256,256]{1,0:T(8,128)S(1)} %get-tuple-element.4, f32[256,256]{1,0:T(8,128)S(1)} %fusion.46), kind=kOutput, calls=%fused_computation.3 | convolution fusion | flops 806354688 | bytes 1836032 | tf_op jit(solution)/shard_map/dot_general | solution.py:84
  122.1 1.9 %fusion.1 = f32[256]{0:T(256)S(1)} fusion(f32[256,512]{1,0:T(8,128)S(1)} %copy.19, f32[256,512]{0,1:T(8,128)S(1)} %bitcast.43, f32[256,256]{1,0:T(8,128)S(1)} %get-tuple-element.3, f32[256,256]{1,0:T(8,128)S(1)} %get-tuple-element.2, f32[256,256]{1,0:T(8,128)S(1)} %fusion.47), kind=kOutput, calls=%fused_computation.4 | convolution fusion | flops 806354688 | bytes 1836032 | tf_op jit(solution)/shard_map/dot_general | solution.py:88
  124.0 0.1 fusion.43
  124.1 0.6 add_divide_fusion
  (8 shorter events, 0.2 us)
Async XLA Ops:
  0.6 32.6 %copy-start = (f32[2,8,16,512]{3,2,1,0:T(8,128)S(1)}, f32[2,8,16,512]{3,2,1,0:T(8,128)}, u32[]{:S(2)}) copy-start(f32[2,8,16,512]{3,2,1,0:T(8,128)} %param.5) | copy-start | bytes 1572868
  0.6 41.5 %copy-start.3 = (f32[16,512]{1,0:T(8,128)S(1)}, f32[16,512]{1,0:T(8,128)}, u32[]{:S(2)}) copy-start(f32[16,512]{1,0:T(8,128)} %param.6) | copy-start | bytes 98308
  1.8 15.3 %collective-permute-start = (f32[2,8,1,512]{3,2,1,0:T(1,128)S(1)}, f32[2,8,1,512]{3,2,1,0:T(1,128)S(1)}, u32[]{:S(2)}, u32[]{:S(2)}) collective-permute-start(f32[2,8,1,512]{3,2,1,0:T(1,128)S(1)} %get-tuple-element.20), channel_id=1, source_target_pairs={{1,0},{2,1},{3,2},{4,3},{5,4},{6,5},{7,6},{8,7},{9,8},{10,9},{11,1... | collective-permute-start | bytes 98312 | tf_op jit(solution)/shard_map/ppermute | solution.py:24
  12.4 6.8 %collective-permute-start.1 = (f32[2,8,1,512]{3,2,1,0:T(1,128)S(1)}, f32[2,8,1,512]{3,2,1,0:T(1,128)S(1)}, u32[]{:S(2)}, u32[]{:S(2)}) collective-permute-start(f32[2,8,1,512]{3,2,1,0:T(1,128)S(1)} %get-tuple-element.21), channel_id=1, source_target_pairs={{0,1},{1,2},{2,3},{3,4},{4,5},{5,6},{6,7},{7,8},{8,9},{9,10},{10,1... | collective-permute-start | bytes 98312 | tf_op jit(solution)/shard_map/ppermute | solution.py:22
  21.7 5.5 %collective-permute-start.2 = (f32[2,8,1,512]{3,2,1,0:T(1,128)S(1)}, f32[2,8,1,512]{3,2,1,0:T(1,128)S(1)}, u32[]{:S(2)}, u32[]{:S(2)}) collective-permute-start(f32[2,8,1,512]{3,2,1,0:T(1,128)S(1)} %get-tuple-element.16), channel_id=1, source_target_pairs={{1,0},{2,1},{3,2},{4,3},{5,4},{6,5},{7,6},{8,7},{9,8},{10,9},{11,1... | collective-permute-start | bytes 98312 | tf_op jit(solution)/shard_map/ppermute | solution.py:24
  25.2 6.8 %collective-permute-start.3 = (f32[2,8,1,512]{3,2,1,0:T(1,128)S(1)}, f32[2,8,1,512]{3,2,1,0:T(1,128)S(1)}, u32[]{:S(2)}, u32[]{:S(2)}) collective-permute-start(f32[2,8,1,512]{3,2,1,0:T(1,128)S(1)} %get-tuple-element.17), channel_id=1, source_target_pairs={{0,1},{1,2},{2,3},{3,4},{4,5},{5,6},{6,7},{7,8},{8,9},{9,10},{10,1... | collective-permute-start | bytes 98312 | tf_op jit(solution)/shard_map/ppermute | solution.py:22
  33.4 5.3 %collective-permute-start.4 = (f32[2,8,1,512]{3,2,1,0:T(1,128)S(1)}, f32[2,8,1,512]{3,2,1,0:T(1,128)S(1)}, u32[]{:S(2)}, u32[]{:S(2)}) collective-permute-start(f32[2,8,1,512]{3,2,1,0:T(1,128)S(1)} %get-tuple-element.12), channel_id=1, source_target_pairs={{1,0},{2,1},{3,2},{4,3},{5,4},{6,5},{7,6},{8,7},{9,8},{10,9},{11,1... | collective-permute-start | bytes 98312 | tf_op jit(solution)/shard_map/ppermute | solution.py:24
  35.4 6.8 %collective-permute-start.5 = (f32[2,8,1,512]{3,2,1,0:T(1,128)S(1)}, f32[2,8,1,512]{3,2,1,0:T(1,128)S(1)}, u32[]{:S(2)}, u32[]{:S(2)}) collective-permute-start(f32[2,8,1,512]{3,2,1,0:T(1,128)S(1)} %get-tuple-element.13), channel_id=1, source_target_pairs={{0,1},{1,2},{2,3},{3,4},{4,5},{5,6},{6,7},{7,8},{8,9},{9,10},{10,1... | collective-permute-start | bytes 98312 | tf_op jit(solution)/shard_map/ppermute | solution.py:22
  42.7 5.4 %collective-permute-start.6 = (f32[2,8,1,512]{3,2,1,0:T(1,128)S(1)}, f32[2,8,1,512]{3,2,1,0:T(1,128)S(1)}, u32[]{:S(2)}, u32[]{:S(2)}) collective-permute-start(f32[2,8,1,512]{3,2,1,0:T(1,128)S(1)} %get-tuple-element.8), channel_id=1, source_target_pairs={{1,0},{2,1},{3,2},{4,3},{5,4},{6,5},{7,6},{8,7},{9,8},{10,9},{11,1... | collective-permute-start | bytes 98312 | tf_op jit(solution)/shard_map/ppermute | solution.py:24
  44.6 6.8 %collective-permute-start.7 = (f32[2,8,1,512]{3,2,1,0:T(1,128)S(1)}, f32[2,8,1,512]{3,2,1,0:T(1,128)S(1)}, u32[]{:S(2)}, u32[]{:S(2)}) collective-permute-start(f32[2,8,1,512]{3,2,1,0:T(1,128)S(1)} %get-tuple-element.9), channel_id=1, source_target_pairs={{0,1},{1,2},{2,3},{3,4},{4,5},{5,6},{6,7},{7,8},{8,9},{9,10},{10,1... | collective-permute-start | bytes 98312 | tf_op jit(solution)/shard_map/ppermute | solution.py:22
  85.1 18.9 %copy-start.1 = (f32[2,256,256]{2,1,0:T(8,128)S(1)}, f32[2,256,256]{2,1,0:T(8,128)}, u32[]{:S(2)}) copy-start(f32[2,256,256]{2,1,0:T(8,128)} %param.7) | copy-start | bytes 1572868
  85.1 18.9 %copy-start.2 = (f32[2,256,256]{2,1,0:T(8,128)S(1)}, f32[2,256,256]{2,1,0:T(8,128)}, u32[]{:S(2)}) copy-start(f32[2,256,256]{2,1,0:T(8,128)} %param.8) | copy-start | bytes 1572868
  89.3 30.6 %all-to-all-start = ((f32[32,256,2,8]{1,3,2,0:T(8,128)}), f32[32,256,2,8]{1,3,2,0:T(8,128)S(1)}, u32[]{:S(2)}, u32[]{:S(2)}) async-start(f32[32,256,2,8]{1,3,2,0:T(8,128)} %copy.17), calls=%async_computation | async-start | bytes 1048576 | tf_op jit(solution)/shard_map/all_to_all | solution.py:80
where the time goes:
time: 125 us
  starting transfers between devices  43.1 us (34%)
  local copies, waits for them, and re-layouts  39 us (31%)
  waiting for transfers between devices  29.2 us (23%)
  other arithmetic  8.59 us (7%)
  matrix products  3.81 us (3%)
    gather x2, local copies, waits for them, and re-layouts, on_device(): jnp.take(cell_table, search_cells[0], axis=0)  32.8 us
    ppermute x4, starting transfers between devices, padded(): lax.ppermute(head, axis, [((i + 1) % count, i) for i in range(ends)])  17.9 us
    all_to_all x1, waiting for transfers between devices, on_device(): lax.all_to_all(picked, 'grp', split_axis=0, concat_axis=3, tiled=True)  15.8 us
    all_to_all x1, starting transfers between devices, on_device(): lax.all_to_all(picked, 'grp', split_axis=0, concat_axis=3, tiled=True)  14.7 us
    ppermute x4, waiting for transfers between devices, padded(): lax.ppermute(tail, axis, [(i, (i + 1) % count) for i in range(ends)])  13.4 us
    ppermute x4, starting transfers between devices, padded(): lax.ppermute(tail, axis, [(i, (i + 1) % count) for i in range(ends)])  10.6 us
    add x4, other arithmetic, apply_operator(): return lap_scale * laplace + medium * center  4.66 us
    reshape x1, local copies, waits for them, and re-layouts, on_device(): cell_table = field.reshape(2 * hydro_dev, slab_rows * cross_cells).T  2.62 us
  transfers between devices with their start and end apart: 9, of which 5 were waited for; matrix products, arithmetic and copies ran while one was open for 2% of the time, Pallas kernels for 0%

commit v1 on v0

v1 whole, which is shorter than its diff:
```python
import jax
import jax.numpy as jnp
from jax import lax
from jax.sharding import PartitionSpec as P

STEPS = 2
RIM = 2 * STEPS

lap_scale = 0.5
first_coef = (0.0, 0.25)
second_coef = (-0.03, -0.02)


def with_rim(cells, axis):
    count = lax.axis_size(axis)
    rows = cells.shape[1]
    above = lax.ppermute(cells[:, rows - RIM :], axis, [(i, i + 1) for i in range(count - 1)])
    below = lax.ppermute(cells[:, :RIM], axis, [(i + 1, i) for i in range(count - 1)])
    return jnp.concatenate([above, cells, below], axis=1)


def apply_operator(field, medium, inside):
    padded = jnp.pad(field, ((0, 0), (1, 1), (1, 1)))
    laplace = (
        padded[:, 2:, 1:-1]
        + padded[:, :-2, 1:-1]
        + padded[:, 1:-1, 2:]
        + padded[:, 1:-1, :-2]
        - 4.0 * field
    )
    return jnp.where(inside, lap_scale * laplace + medium * field, 0.0)


def march(field, first_pass, second_pass):
    half = field.shape[0] // 2
    fr, fi = first_pass[:half], first_pass[half:]
    sr, si = second_pass[:half], second_pass[half:]
    real = field[:half] + (first_coef[0] * fr - first_coef[1] * fi) + (second_coef[0] * sr - second_coef[1] * si)
    imag = field[half:] + (first_coef[1] * fr + first_coef[0] * fi) + (second_coef[1] * sr + second_coef[0] * si)
    return jnp.concatenate([real, imag], axis=0)


def form(matrix, u, v):
    def dot(a, b):
        return jnp.dot(a, b, precision=lax.Precision.HIGHEST)

    both = dot(matrix[0], jnp.concatenate([u, v], axis=1))
    cells = u.shape[1]
    cross = dot(matrix[1], u)
    return jnp.sum(u * both[:, :cells] + v * both[:, cells:] + 2.0 * (v * cross), axis=0)


def on_device(starter, medium, csm, capon_weight, search_cells):
    parts, hydros, slab_rows, cross_cells = starter.shape
    planes = parts * hydros
    packed = jnp.concatenate([starter.reshape(planes, slab_rows, cross_cells), medium[None]], axis=0)
    packed = with_rim(packed, "row")
    field, medium = packed[:planes], packed[planes]
    depth = lax.axis_index("row") * slab_rows - RIM + lax.broadcasted_iota(jnp.int32, medium.shape, 0)
    inside = (depth >= 0) & (depth < lax.axis_size("row") * slab_rows)
    for marching in range(STEPS):
        first_pass = apply_operator(field, medium, inside)
        second_pass = apply_operator(first_pass, medium, inside)
        field = march(field, first_pass, second_pass)
    field = field[:, RIM : RIM + slab_rows]
    owners = lax.axis_size("grp")
    pieces = field.reshape(parts, hydros, owners, -1)
    vectors = lax.all_to_all(pieces, "grp", split_axis=2, concat_axis=1, tiled=True)[:, :, 0]
    u, v = vectors[0], vectors[1]
    power = jnp.sum(u * u + v * v, axis=0) + 1e-06
    bartlett = form(csm, u, v) / power
    capon = power / form(capon_weight, u, v)
    mine = jnp.stack([bartlett, capon], axis=0)
    cells = mine.shape[1]
    copies = jnp.broadcast_to(mine[None], (owners, 2, cells))
    table = lax.all_to_all(copies, "grp", split_axis=0, concat_axis=0, tiled=True)
    table = jnp.swapaxes(table, 0, 1).reshape(2, owners * cells)
    wanted = lax.dynamic_slice(search_cells, (0, lax.axis_index("grp") * cells), (1, cells))[0]
    result = jnp.take(table, wanted, axis=1)
    return (result[0][None, :], result[1][None, :])


def solution(mesh):
    return jax.shard_map(
        on_device,
        mesh=mesh,
        in_specs=(P(None, "grp", "row", None), P("row", None), P(), P(), P("row", None)),
        out_specs=(P("row", "grp"), P("row", "grp")),
        check_vma=False,
    )
```

time: 125 us -> 74.7 us (0.60)
  the two profiles are of different devices: /device:TPU:9 before, /device:TPU:193 now
where the time goes in v1:
time: 74.7 us; the launch traced here: 74.4 us
  waiting for transfers between devices  32.9 us (44%)
  starting transfers between devices  23.6 us (32%)
  local copies, waits for them, and re-layouts  8.8 us (12%)
  other arithmetic  6.01 us (8%)
  matrix products  2.15 us (3%)
  between operations  0.89 us (1%)
    all_to_all x1, waiting for transfers between devices, on_device(): lax.all_to_all(pieces, 'grp', split_axis=2, concat_axis=1, tiled=True)  17.7 us
    all_to_all x1, starting transfers between devices, on_device(): lax.all_to_all(pieces, 'grp', split_axis=2, concat_axis=1, tiled=True)  11.7 us
    all_to_all x1, waiting for transfers between devices, on_device(): lax.all_to_all(copies, 'grp', split_axis=0, concat_axis=0, tiled=True)  9.78 us
    ppermute x1, starting transfers between devices, with_rim(): lax.ppermute(cells[:, rows - RIM:], axis, [(i, i + 1) for i in range(coun...  5.21 us
    ppermute x1, waiting for transfers between devices, with_rim(): lax.ppermute(cells[:, :RIM], axis, [(i + 1, i) for i in range(count - 1)])  5.01 us
    all_to_all x1, starting transfers between devices, on_device(): lax.all_to_all(copies, 'grp', split_axis=0, concat_axis=0, tiled=True)  4.8 us
    gather x1, local copies, waits for them, and re-layouts, on_device(): result = jnp.take(table, wanted, axis=1)  2.91 us
    transpose x1, local copies, waits for them, and re-layouts, on_device(): table = jnp.swapaxes(table, 0, 1).reshape(2, owners * cells)  2.6 us
  transfers between devices with their start and end apart: 4, of which 4 were waited for; matrix products, arithmetic and copies ran while one was open for 1% of the time, Pallas kernels for 0%

profile of v1, /device:TPU:193, one launch (start us, length us, event | category | flops | bytes accessed | tf_op | source)
XLA Modules:
  0.0 74.4 jit_solution(12616035583715683622)
XLA Ops:
  0.6 1.1 %pad_maximum_fusion.7 = (f32[17,4,512]{2,1,0:T(4,128)S(1)}, f32[17,4,512]{2,1,0:T(4,128)S(1)}) fusion(f32[1,16,512]{2,1,0:T(8,128)} %bitcast.76, f32[16,16,512]{2,1,0:T(8,128)} %bitcast.69), kind=kLoop, calls=%fused_computation.85 | loop fusion | flops 69632 | bytes 835584 | tf_op jit(solution)/shard_map/slice | solution.py:17
  1.8 5.2 %collective-permute-start = (f32[17,4,512]{2,1,0:T(4,128)S(1)}, f32[17,4,512]{2,1,0:T(4,128)S(1)}, u32[]{:S(2)}, u32[]{:S(2)}) collective-permute-start(f32[17,4,512]{2,1,0:T(4,128)S(1)} %get-tuple-element.14), channel_id=1, source_target_pairs={{0,1},{1,2},{2,3},{3,4},{4,5},{5,6},{6,7},{7,8},{8,9},{9,10},{10,1... | collective-permute-start | bytes 417800 | tf_op jit(solution)/shard_map/ppermute | solution.py:17
  7.0 1.9 %collective-permute-start.1 = (f32[17,4,512]{2,1,0:T(4,128)S(1)}, f32[17,4,512]{2,1,0:T(4,128)S(1)}, u32[]{:S(2)}, u32[]{:S(2)}) collective-permute-start(f32[17,4,512]{2,1,0:T(4,128)S(1)} %get-tuple-element.15), channel_id=1, source_target_pairs={{1,0},{2,1},{3,2},{4,3},{5,4},{6,5},{7,6},{8,7},{9,8},{10,9},{11,1... | collective-permute-start | bytes 417800 | tf_op jit(solution)/shard_map/ppermute | solution.py:18
  8.9 0.0 copy-start
  8.9 0.0 copy-start.1
  8.9 0.3 collective-permute-done
  9.3 5.0 %collective-permute-done.1 = f32[17,4,512]{2,1,0:T(4,128)S(1)} collective-permute-done((f32[17,4,512]{2,1,0:T(4,128)S(1)}, f32[17,4,512]{2,1,0:T(4,128)S(1)}, u32[]{:S(2)}, u32[]{:S(2)}) %collective-permute-start.1) | collective-permute-done | bytes 139296 | tf_op jit(solution)/shard_map/ppermute | solution.py:18
  14.3 1.2 %pad_maximum_fusion = f32[17,24,512]{2,1,0:T(8,128)S(1)} fusion(f32[17,4,512]{2,1,0:T(4,128)S(1)} %collective-permute-done.1, f32[1,16,512]{2,1,0:T(8,128)} %bitcast.77, f32[16,16,512]{2,1,0:T(8,128)} %bitcast.70, f32[17,4,512]{2,1,0:T(4,128)S(1)} %collective-permute-done), kind=kLoop, calls=%fused_computation.29 | loop fusion | flops 626688 | bytes 1671168 | tf_op jit(solution)/shard_map/concatenate | solution.py:19
  15.5 0.1 slice.179
  15.6 0.0 copy-done
  15.6 0.0 copy-done.1
  15.6 0.5 fusion.14
  16.1 0.5 fusion.21
  16.7 0.3 fusion.37
  17.0 0.1 pad_maximum_fusion.1
  17.0 0.5 fusion.28
  17.5 0.5 fusion.35
  18.1 0.3 subtract_add_fusion
  18.4 0.1 pad_maximum_fusion.2
  18.4 0.1 reshape.83
  18.5 1.1 %copy.14 = f32[2,8,32,256]{3,1,0,2:T(8,128)} copy(f32[2,8,32,256]{3,2,1,0:T(8,128)S(1)} %reshape.83) | data formatting | bytes 1048576 | tf_op jit(solution)/shard_map/reshape | solution.py:67
  19.6 0.0 copy-start.2
  19.6 11.7 %all-to-all-start = ((f32[2,8,32,256]{3,1,0,2:T(8,128)}), f32[2,8,32,256]{3,1,0,2:T(8,128)S(1)}, u32[]{:S(2)}, u32[]{:S(2)}) async-start(f32[2,8,32,256]{3,1,0,2:T(8,128)} %copy.14), calls=%async_computation | async-start | bytes 1048576 | tf_op jit(solution)/shard_map/all_to_all | solution.py:68
  31.4 0.7 compare_select_fusion
  32.1 17.7 %all-to-all-done = f32[2,8,32,256]{3,1,0,2:T(8,128)S(1)} async-done(((f32[2,8,32,256]{3,1,0,2:T(8,128)}), f32[2,8,32,256]{3,1,0,2:T(8,128)S(1)}, u32[]{:S(2)}, u32[]{:S(2)}) %all-to-all-start) | async-done | bytes 524320 | tf_op jit(solution)/shard_map/all_to_all | solution.py:68
  49.8 0.1 add_reduce_fusion
  49.9 0.0 copy-start.3
  49.9 0.0 copy-done.2
  49.9 0.6 convolution_bitcast_fusion
  50.5 0.4 fusion.6
  51.0 0.0 copy-done.3
  51.0 0.6 convolution_bitcast_fusion.1
  51.6 0.4 fusion.7
  52.1 0.6 broadcast_in_dim.37
  52.7 4.8 %all-to-all-start.1 = ((f32[32,2,256]{2,1,0:T(2,128)}), f32[32,2,256]{2,1,0:T(2,128)S(1)}, u32[]{:S(2)}, u32[]{:S(2)}) async-start(f32[32,2,256]{2,1,0:T(2,128)} %broadcast_in_dim.37), calls=%async_computation.1 | async-start | bytes 131072 | tf_op jit(solution)/shard_map/all_to_all | solution.py:76
  57.6 9.8 %all-to-all-done.1 = f32[32,2,256]{2,1,0:T(2,128)S(1)} async-done(((f32[32,2,256]{2,1,0:T(2,128)}), f32[32,2,256]{2,1,0:T(2,128)S(1)}, u32[]{:S(2)}, u32[]{:S(2)}) %all-to-all-start.1) | async-done | bytes 65568 | tf_op jit(solution)/shard_map/all_to_all | solution.py:76
  67.4 2.6 %copy.15 = f32[2,32,256]{0,2,1:T(8,128)} copy(f32[2,32,256]{2,0,1:T(2,128)S(1)} %bitcast.79) | data formatting | bytes 131072 | tf_op jit(solution)/shard_map/transpose | solution.py:77
  70.0 2.9 %gather_fusion = f32[256,2]{1,0:T(8,128)S(1)} fusion(f32[2,8192]{0,1:T(8,128)} %bitcast.72, s32[1024]{0:T(1024)S(1)} %pad_clamp_fusion), kind=kCustom, calls=%fused_computation | custom fusion | bytes 5120 | tf_op jit(solution)/shard_map/jit(_take)/gather | solution.py:79
  72.9 0.1 select_bitcast_fusion
  73.0 0.1 fusion.50
  73.1 0.6 copy.17
  73.7 0.6 copy.16
  (6 shorter events, 0.1 us)
Async XLA Ops:
  1.8 7.5 %collective-permute-start = (f32[17,4,512]{2,1,0:T(4,128)S(1)}, f32[17,4,512]{2,1,0:T(4,128)S(1)}, u32[]{:S(2)}, u32[]{:S(2)}) collective-permute-start(f32[17,4,512]{2,1,0:T(4,128)S(1)} %get-tuple-element.14), channel_id=1, source_target_pairs={{0,1},{1,2},{2,3},{3,4},{4,5},{5,6},{6,7},{7,8},{8,9},{9,10},{10,1... | collective-permute-start | bytes 417800 | tf_op jit(solution)/shard_map/ppermute | solution.py:17
  7.0 7.3 %collective-permute-start.1 = (f32[17,4,512]{2,1,0:T(4,128)S(1)}, f32[17,4,512]{2,1,0:T(4,128)S(1)}, u32[]{:S(2)}, u32[]{:S(2)}) collective-permute-start(f32[17,4,512]{2,1,0:T(4,128)S(1)} %get-tuple-element.15), channel_id=1, source_target_pairs={{1,0},{2,1},{3,2},{4,3},{5,4},{6,5},{7,6},{8,7},{9,8},{10,9},{11,1... | collective-permute-start | bytes 417800 | tf_op jit(solution)/shard_map/ppermute | solution.py:18
  8.9 6.6 %copy-start = (f32[2,8,16,512]{3,2,1,0:T(8,128)S(1)}, f32[2,8,16,512]{3,2,1,0:T(8,128)}, u32[]{:S(2)}) copy-start(f32[2,8,16,512]{3,2,1,0:T(8,128)} %param.5) | copy-start | bytes 1572868
  8.9 6.6 %copy-start.1 = (f32[16,512]{1,0:T(8,128)S(1)}, f32[16,512]{1,0:T(8,128)}, u32[]{:S(2)}) copy-start(f32[16,512]{1,0:T(8,128)} %param.6) | copy-start | bytes 98308
  19.6 30.2 %copy-start.2 = (f32[2,256,256]{2,1,0:T(8,128)S(1)}, f32[2,256,256]{2,1,0:T(8,128)}, u32[]{:S(2)}) copy-start(f32[2,256,256]{2,1,0:T(8,128)} %param.8) | copy-start | bytes 1572868
  19.6 30.1 %all-to-all-start = ((f32[2,8,32,256]{3,1,0,2:T(8,128)}), f32[2,8,32,256]{3,1,0,2:T(8,128)S(1)}, u32[]{:S(2)}, u32[]{:S(2)}) async-start(f32[2,8,32,256]{3,1,0,2:T(8,128)} %copy.14), calls=%async_computation | async-start | bytes 1048576 | tf_op jit(solution)/shard_map/all_to_all | solution.py:68
  49.9 1.1 %copy-start.3 = (f32[2,256,256]{2,1,0:T(8,128)S(1)}, f32[2,256,256]{2,1,0:T(8,128)}, u32[]{:S(2)}) copy-start(f32[2,256,256]{2,1,0:T(8,128)} %param.7) | copy-start | bytes 1572868
  52.7 14.6 %all-to-all-start.1 = ((f32[32,2,256]{2,1,0:T(2,128)}), f32[32,2,256]{2,1,0:T(2,128)S(1)}, u32[]{:S(2)}, u32[]{:S(2)}) async-start(f32[32,2,256]{2,1,0:T(2,128)} %broadcast_in_dim.37), calls=%async_computation.1 | async-start | bytes 131072 | tf_op jit(solution)/shard_map/all_to_all | solution.py:76

commit v2 on v1

v2 whole, which is shorter than its diff:
```python
import functools

import jax
import jax.numpy as jnp
from jax import lax
from jax.experimental import pallas as pl
from jax.experimental.pallas import tpu as pltpu
from jax.sharding import PartitionSpec as P

STEPS = 2
RIM = 2 * STEPS
LANES = 128
MESH = pl.DeviceIdType.MESH

first_imag = 0.25
second_coef = (-0.03, -0.02)


def kernel(
    owners, slabs, rows,
    starter_ref, medium_ref, csm_ref, weight_ref, cells_ref,
    bartlett_ref, capon_ref,
    start, field, first, middle, coef, medium_above, medium_below,
    outgoing, vectors, csm, weight, mine, table,
    start_sem, local_sem, rim_send, rim_recv, block_send, block_recv, result_send, result_recv,
):
    me = lax.axis_index("grp")
    slab = lax.axis_index("row")
    above = lax.rem(slab + slabs - 1, slabs)
    below = lax.rem(slab + 1, slabs)
    hydros, cols = field.shape[2:]
    tiles = cols // LANES
    inner = rows // 2

    barrier = pltpu.get_barrier_semaphore()
    for other in (above, below):
        pl.semaphore_signal(barrier, inc=1, device_id={"row": other}, device_id_type=MESH)

    @pl.loop(1, owners)
    def _(step):
        other = lax.rem(me + step, owners)
        pl.semaphore_signal(barrier, inc=1, device_id={"grp": other}, device_id_type=MESH)

    loads = []
    for t in range(tiles):
        load = pltpu.make_async_copy(
            starter_ref.at[:, :, t * LANES : (t + 1) * LANES], start.at[t], start_sem.at[t]
        )
        load.start()
        loads.append(load)
    load_csm = pltpu.make_async_copy(csm_ref, csm, local_sem.at[1])
    load_csm.start()
    load_weight = pltpu.make_async_copy(weight_ref, weight, local_sem.at[2])
    load_weight.start()

    def spread(ref, r):
        return jnp.broadcast_to(ref[r : r + 1, :], (hydros, cols)) - 2.0

    for r in range(rows):
        coef[RIM + r] = spread(medium_ref, r)
    for t in range(tiles):
        loads[t].wait()
        for part in range(2):
            for r in range(rows):
                field[part, RIM + r, :, t * LANES : (t + 1) * LANES] = start[
                    t, part, pl.ds(r, hydros, stride=rows), :
                ]

    col = lax.broadcasted_iota(jnp.int32, (hydros, cols), 1)

    def operate(ref, part, r, half):
        here = ref[part, r]
        left = jnp.where(col == 0, 0.0, pltpu.roll(here, 1, 1))
        right = jnp.where(col == cols - 1, 0.0, pltpu.roll(here, cols - 1, 1))
        total = (ref[part, r - 1] + ref[part, r + 1]) + (left + right)
        return half * total + coef[r] * here

    def scale(r):
        outside = ((slab == 0) & (r < RIM)) | ((slab == slabs - 1) & (r >= RIM + rows))
        return jnp.where(outside, 0.0, 0.5).astype(jnp.float32)

    def apply_first(source, r):
        half = scale(r)
        for part in range(2):
            first[part, r] = operate(source, part, r, half)

    def advance(source, r):
        half = scale(r)
        fr, fi = first[0, r], first[1, r]
        sr = operate(first, 0, r, half)
        si = operate(first, 1, r, half)
        real = source[0, r] - first_imag * fi + second_coef[0] * sr - second_coef[1] * si
        imag = source[1, r] + first_imag * fr + second_coef[1] * sr + second_coef[0] * si
        return real, imag

    def first_one(r):
        apply_first(field, r)

    def step_one(r):
        real, imag = advance(field, r)
        middle[0, r] = real
        middle[1, r] = imag

    def first_two(r):
        apply_first(middle, r)

    def step_two(block, base, r):
        real, imag = advance(middle, r)
        for t in range(tiles):
            owner = (r - base) * tiles + t
            outgoing[block, owner, 0] = real[:, t * LANES : (t + 1) * LANES]
            outgoing[block, owner, 1] = imag[:, t * LANES : (t + 1) * LANES]

    def loop(low, high, body):
        lax.fori_loop(low, high, lambda r, c: (body(r), c)[1], 0)

    loop(RIM + 1, RIM + rows - 1, first_one)
    loop(RIM + 2, RIM + rows - 2, step_one)
    loop(RIM + 3, RIM + rows - 3, first_two)
    loop(RIM + 4, RIM + rows - 4, functools.partial(step_two, 0, RIM + 4))

    pl.semaphore_wait(barrier, owners + 1)

    def rim_copy(k, source, target, other):
        return pltpu.make_async_remote_copy(
            src_ref=source, dst_ref=target, send_sem=rim_send.at[k], recv_sem=rim_recv.at[k],
            device_id={"row": other}, device_id_type=MESH,
        )

    rims = [
        rim_copy(0, field.at[:, pl.ds(RIM, RIM)], field.at[:, pl.ds(RIM + rows, RIM)], above),
        rim_copy(1, field.at[:, pl.ds(rows, RIM)], field.at[:, pl.ds(0, RIM)], below),
        rim_copy(2, medium_ref.at[pl.ds(0, 8)], medium_below, above),
        rim_copy(3, medium_ref.at[pl.ds(rows - 8, 8)], medium_above, below),
    ]
    for copy in rims:
        copy.start()

    def block_copy(block, source, target):
        return pltpu.make_async_remote_copy(
            src_ref=outgoing.at[block, target], dst_ref=vectors.at[block, source],
            send_sem=block_send.at[block, target], recv_sem=block_recv.at[block, source],
            device_id={"grp": target}, device_id_type=MESH,
        )

    def send_blocks(block):
        @pl.loop(1, owners)
        def _(step):
            block_copy(block, me, lax.rem(me + step, owners)).start()

        own = pltpu.make_async_copy(
            outgoing.at[block, me], vectors.at[block, me], local_sem.at[3 + block]
        )
        own.start()
        return own

    own_inner = send_blocks(0)

    for copy in rims:
        copy.wait_recv()

    @pl.when(slab == 0)
    def _():
        field[:, 0:RIM] = jnp.zeros((2, RIM, hydros, cols), jnp.float32)

    @pl.when(slab == slabs - 1)
    def _():
        field[:, RIM + rows :] = jnp.zeros((2, RIM, hydros, cols), jnp.float32)

    for r in range(RIM):
        coef[r] = spread(medium_above, 8 - RIM + r)
        coef[RIM + rows + r] = spread(medium_below, r)

    top = RIM + rows
    loop(1, 5, first_one)
    loop(top - 1, top + 3, first_one)
    loop(2, 6, step_one)
    loop(top - 2, top + 2, step_one)
    loop(3, 7, first_two)
    loop(top - 3, top + 1, first_two)
    loop(4, 8, functools.partial(step_two, 1, RIM))
    loop(top - 4, top, functools.partial(step_two, 1, RIM + inner))

    own_outer = send_blocks(1)

    load_csm.wait()
    load_weight.wait()
    own_inner.wait()
    own_outer.wait()
    for block in range(2):
        @pl.loop(1, owners)
        def _(step):
            block_copy(block, lax.rem(me + step, owners), me).wait_recv()

    def stacked(part):
        return jnp.concatenate(
            [vectors[block, :, part].reshape(owners * hydros, LANES) for block in range(2)], axis=1
        )

    u, v = stacked(0), stacked(1)
    power = jnp.sum(u * u + v * v, axis=0, keepdims=True) + 1e-06

    def form(matrix):
        def dot(a, b):
            return jnp.dot(
                a, b, precision=lax.Precision.HIGHEST, preferred_element_type=jnp.float32
            )

        return jnp.sum(
            u * dot(matrix[0], u) + v * (dot(matrix[0], v) + 2.0 * dot(matrix[1], u)),
            axis=0, keepdims=True,
        )

    bartlett = form(csm) / power
    capon = power / form(weight)
    mine[0:1] = bartlett[:, :LANES]
    mine[1:2] = bartlett[:, LANES:]
    mine[2:3] = capon[:, :LANES]
    mine[3:4] = capon[:, LANES:]

    def result_copy(source, target):
        return pltpu.make_async_remote_copy(
            src_ref=mine, dst_ref=table.at[source],
            send_sem=result_send.at[target], recv_sem=result_recv.at[source],
            device_id={"grp": target}, device_id_type=MESH,
        )

    @pl.loop(1, owners)
    def _(step):
        result_copy(me, lax.rem(me + step, owners)).start()

    own_result = pltpu.make_async_copy(mine, table.at[me], local_sem.at[5])
    own_result.start()

    share = bartlett_ref.shape[1]
    wanted = cells_ref[:, pl.ds(pl.multiple_of(me * share, share), share)]
    tile = wanted // LANES
    lane = wanted - tile * LANES
    edge = (inner // 2) * tiles
    is_inner = (tile >= edge) & (tile < edge + owners)
    owner = jnp.where(is_inner, tile - edge, jnp.where(tile < edge, tile, tile - owners))
    entry = owner * 4 + jnp.where(is_inner, 0, 1)
    place = lax.broadcasted_iota(jnp.int32, (owners * 4, share), 0)
    pick_bartlett = jnp.where(place == entry, 1.0, 0.0)
    pick_capon = jnp.where(place == entry + 2, 1.0, 0.0)
    on_lane = lax.broadcasted_iota(jnp.int32, (LANES, share), 0) == lane

    own_result.wait()

    @pl.loop(1, owners)
    def _(step):
        result_copy(lax.rem(me + step, owners), me).wait_recv()

    flat = table[...].reshape(owners * 4, LANES).T

    def take(pick):
        chosen = jnp.dot(
            flat, pick, precision=lax.Precision.HIGHEST, preferred_element_type=jnp.float32
        )
        return jnp.sum(jnp.where(on_lane, chosen, 0.0), axis=0, keepdims=True)

    bartlett_ref[...] = take(pick_bartlett)
    capon_ref[...] = take(pick_capon)

    for copy in rims:
        copy.wait_send()

    @pl.loop(1, owners)
    def _(step):
        other = lax.rem(me + step, owners)
        block_copy(0, me, other).wait_send()
        block_copy(1, me, other).wait_send()
        result_copy(me, other).wait_send()


def on_device(starter, medium, csm, capon_weight, search_cells):
    parts, hydros, rows, cols = starter.shape
    owners = lax.axis_size("grp")
    slabs = lax.axis_size("row")
    depth = rows + 2 * RIM
    share = search_cells.shape[1] // owners
    vmem = pl.BlockSpec(memory_space=pltpu.VMEM)
    anywhere = pl.BlockSpec(memory_space=pl.ANY)
    plane = pltpu.VMEM((parts, depth, hydros, cols), jnp.float32)
    blocks = pltpu.VMEM((2, owners, parts, hydros, LANES), jnp.float32)
    return pl.pallas_call(
        functools.partial(kernel, owners, slabs, rows),
        out_shape=[jax.ShapeDtypeStruct((1, share), jnp.float32)] * 2,
        in_specs=[anywhere, vmem, anywhere, anywhere, vmem],
        out_specs=[vmem, vmem],
        scratch_shapes=[
            pltpu.VMEM((cols // LANES, parts, hydros * rows, LANES), jnp.float32),
            plane,
            plane,
            plane,
            pltpu.VMEM((depth, hydros, cols), jnp.float32),
            pltpu.VMEM((8, cols), jnp.float32),
            pltpu.VMEM((8, cols), jnp.float32),
            blocks,
            blocks,
            pltpu.VMEM(csm.shape, jnp.float32),
            pltpu.VMEM(csm.shape, jnp.float32),
            pltpu.VMEM((4, LANES), jnp.float32),
            pltpu.VMEM((owners, 4, LANES), jnp.float32),
            pltpu.SemaphoreType.DMA((cols // LANES,)),
            pltpu.SemaphoreType.DMA((6,)),
            pltpu.SemaphoreType.DMA((4,)),
            pltpu.SemaphoreType.DMA((4,)),
            pltpu.SemaphoreType.DMA((2, owners)),
            pltpu.SemaphoreType.DMA((2, owners)),
            pltpu.SemaphoreType.DMA((owners,)),
            pltpu.SemaphoreType.DMA((owners,)),
        ],
        compiler_params=pltpu.CompilerParams(collective_id=0, has_side_effects=True),
    )(starter.reshape(parts, hydros * rows, cols), medium, csm, capon_weight, search_cells)


def solution(mesh):
    return jax.shard_map(
        on_device,
        mesh=mesh,
        in_specs=(P(None, "grp", "row", None), P("row", None), P(), P(), P("row", None)),
        out_specs=(P("row", "grp"), P("row", "grp")),
        check_vma=False,
    )
```

time: 74.7 us -> 51.6 us (0.69)
  the two profiles are of different devices: /device:TPU:193 before, /device:TPU:1 now
where the time goes in v2:
time: 51.6 us; the launch traced here: 51.4 us
  Pallas kernels  48.9 us (95%)
  local copies, waits for them, and re-layouts  1.85 us (4%)
  between operations  0.65 us (1%)
    pallas_call x1, Pallas kernels, on_device(): pl.pallas_call(functools.partial(kernel, owners, slabs, rows), out_shape=...  48.9 us
    unnamed x6, local copies, waits for them, and re-layouts  1.85 us

profile of v2, /device:TPU:1, one launch (start us, length us, event | category | flops | bytes accessed | tf_op | source)
XLA Modules:
  0.0 51.4 jit_solution(6173174687158117057)
XLA Ops:
  0.6 48.9 %shard_map.68 = (f32[1,256]{1,0:T(1,128)}, f32[1,256]{1,0:T(1,128)}) custom-call(f32[2,128,512]{2,1,0:T(8,128)} %bitcast.1, f32[16,512]{1,0:T(8,128)} %medium_ref.1, f32[2,256,256]{2,1,0:T(8,128)} %csm_ref.1, f32[2,256,256]{2,1,0:T(8,128)} %weight_ref.1, s32[1,8192]{1,0:T(1,128)} %cells_ref.1), custom_call_target="tpu_custom_call" | custom-call | tf_op jit(solution)/shard_map/pallas_call | solution.py:286
  49.5 0.0 copy-start.1
  49.5 0.7 %copy-done.1 = f32[1,256]{1,0:T(1,128)S(1)} copy-done((f32[1,256]{1,0:T(1,128)S(1)}, f32[1,256]{1,0:T(1,128)}, u32[]{:S(2)}) %copy-start.1) | copy-done | bytes 1048
  50.2 0.0 copy-start
  50.2 0.6 %copy.9 = f32[1,256]{1,0:T(1,128)} copy(f32[1,256]{1,0:T(1,128)S(1)} %copy-done.1) | data formatting | bytes 2048
  50.8 0.1 copy-done
  50.8 0.6 %copy.10 = f32[1,256]{1,0:T(1,128)} copy(f32[1,256]{1,0:T(1,128)S(1)} %copy-done) | data formatting | bytes 2048
Async XLA Ops:
  49.5 0.7 %copy-start.1 = (f32[1,256]{1,0:T(1,128)S(1)}, f32[1,256]{1,0:T(1,128)}, u32[]{:S(2)}) copy-start(f32[1,256]{1,0:T(1,128)} %get-tuple-element.4) | copy-start | bytes 3076
  50.2 0.6 %copy-start = (f32[1,256]{1,0:T(1,128)S(1)}, f32[1,256]{1,0:T(1,128)}, u32[]{:S(2)}) copy-start(f32[1,256]{1,0:T(1,128)} %get-tuple-element.5) | copy-start | bytes 3076

commit v3 on v2

--- a/solution.py
+++ b/solution.py
@@ -19,7 +19,7 @@
 def kernel(
     owners, slabs, rows,
     starter_ref, medium_ref, csm_ref, weight_ref, cells_ref,
-    bartlett_ref, capon_ref,
+    result_ref,
     start, field, first, middle, coef, medium_above, medium_below,
     outgoing, vectors, csm, weight, mine, table,
     start_sem, local_sem, rim_send, rim_recv, block_send, block_recv, result_send, result_recv,
@@ -49,22 +49,22 @@
         load.start()
         loads.append(load)
     load_csm = pltpu.make_async_copy(csm_ref, csm, local_sem.at[1])
-    load_csm.start()
     load_weight = pltpu.make_async_copy(weight_ref, weight, local_sem.at[2])
-    load_weight.start()
 
     def spread(ref, r):
         return jnp.broadcast_to(ref[r : r + 1, :], (hydros, cols)) - 2.0
 
-    for r in range(rows):
-        coef[RIM + r] = spread(medium_ref, r)
-    for t in range(tiles):
-        loads[t].wait()
-        for part in range(2):
-            for r in range(rows):
-                field[part, RIM + r, :, t * LANES : (t + 1) * LANES] = start[
-                    t, part, pl.ds(r, hydros, stride=rows), :
-                ]
+    def place_rows(which):
+        for t in range(tiles):
+            for part in range(2):
+                for r in which:
+                    field[part, RIM + r, :, t * LANES : (t + 1) * LANES] = start[
+                        t, part, pl.ds(r, hydros, stride=rows), :
+                    ]
+
+    for load in loads:
+        load.wait()
+    place_rows([*range(RIM), *range(rows - RIM, rows)])
 
     col = lax.broadcasted_iota(jnp.int32, (hydros, cols), 1)
 
@@ -76,7 +76,9 @@
         return half * total + coef[r] * here
 
     def scale(r):
-        outside = ((slab == 0) & (r < RIM)) | ((slab == slabs - 1) & (r >= RIM + rows))
+        if not isinstance(r, int) or RIM <= r < RIM + rows:
+            return 0.5
+        outside = slab == (0 if r < RIM else slabs - 1)
         return jnp.where(outside, 0.0, 0.5).astype(jnp.float32)
 
     def apply_first(source, r):
@@ -111,14 +113,6 @@
             outgoing[block, owner, 0] = real[:, t * LANES : (t + 1) * LANES]
             outgoing[block, owner, 1] = imag[:, t * LANES : (t + 1) * LANES]
 
-    def loop(low, high, body):
-        lax.fori_loop(low, high, lambda r, c: (body(r), c)[1], 0)
-
-    loop(RIM + 1, RIM + rows - 1, first_one)
-    loop(RIM + 2, RIM + rows - 2, step_one)
-    loop(RIM + 3, RIM + rows - 3, first_two)
-    loop(RIM + 4, RIM + rows - 4, functools.partial(step_two, 0, RIM + 4))
-
     pl.semaphore_wait(barrier, owners + 1)
 
     def rim_copy(k, source, target, other):
@@ -154,6 +148,25 @@
         own.start()
         return own
 
+    load_csm.start()
+    load_weight.start()
+    place_rows(range(RIM, rows - RIM))
+    for r in range(rows):
+        coef[RIM + r] = spread(medium_ref, r)
+
+    def pairs(low, high, body):
+        def both(i, carry):
+            body(low + 2 * i)
+            body(low + 2 * i + 1)
+            return carry
+
+        lax.fori_loop(0, (high - low) // 2, both, 0)
+
+    pairs(RIM + 1, RIM + rows - 1, first_one)
+    pairs(RIM + 2, RIM + rows - 2, step_one)
+    pairs(RIM + 3, RIM + rows - 3, first_two)
+    pairs(RIM + 4, RIM + rows - 4, functools.partial(step_two, 0, RIM + 4))
+
     own_inner = send_blocks(0)
 
     for copy in rims:
@@ -172,14 +185,13 @@
         coef[RIM + rows + r] = spread(medium_below, r)
 
     top = RIM + rows
-    loop(1, 5, first_one)
-    loop(top - 1, top + 3, first_one)
-    loop(2, 6, step_one)
-    loop(top - 2, top + 2, step_one)
-    loop(3, 7, first_two)
-    loop(top - 3, top + 1, first_two)
-    loop(4, 8, functools.partial(step_two, 1, RIM))
-    loop(top - 4, top, functools.partial(step_two, 1, RIM + inner))
+    for stage, body in enumerate((first_one, step_one, first_two)):
+        for r in range(RIM):
+            body(1 + stage + r)
+            body(top - 1 - stage + r)
+    for r in range(RIM):
+        step_two(1, RIM, RIM + r)
+        step_two(1, RIM + inner, top - RIM + r)
 
     own_outer = send_blocks(1)
 
@@ -232,7 +244,7 @@
     own_result = pltpu.make_async_copy(mine, table.at[me], local_sem.at[5])
     own_result.start()
 
-    share = bartlett_ref.shape[1]
+    share = result_ref.shape[1]
     wanted = cells_ref[:, pl.ds(pl.multiple_of(me * share, share), share)]
     tile = wanted // LANES
     lane = wanted - tile * LANES
@@ -259,8 +271,8 @@
         )
         return jnp.sum(jnp.where(on_lane, chosen, 0.0), axis=0, keepdims=True)
 
-    bartlett_ref[...] = take(pick_bartlett)
-    capon_ref[...] = take(pick_capon)
+    result_ref[0:1] = take(pick_bartlett)
+    result_ref[1:2] = take(pick_capon)
 
     for copy in rims:
         copy.wait_send()
@@ -283,11 +295,11 @@
     anywhere = pl.BlockSpec(memory_space=pl.ANY)
     plane = pltpu.VMEM((parts, depth, hydros, cols), jnp.float32)
     blocks = pltpu.VMEM((2, owners, parts, hydros, LANES), jnp.float32)
-    return pl.pallas_call(
+    result = pl.pallas_call(
         functools.partial(kernel, owners, slabs, rows),
-        out_shape=[jax.ShapeDtypeStruct((1, share), jnp.float32)] * 2,
+        out_shape=jax.ShapeDtypeStruct((2, share), jnp.float32),
         in_specs=[anywhere, vmem, anywhere, anywhere, vmem],
-        out_specs=[vmem, vmem],
+        out_specs=vmem,
         scratch_shapes=[
             pltpu.VMEM((cols // LANES, parts, hydros * rows, LANES), jnp.float32),
             plane,
@@ -313,6 +325,7 @@
         ],
         compiler_params=pltpu.CompilerParams(collective_id=0, has_side_effects=True),
     )(starter.reshape(parts, hydros * rows, cols), medium, csm, capon_weight, search_cells)
+    return result[0:1], result[1:2]
 
 
 def solution(mesh):

time: 51.6 us -> 48.2 us (0.934)
  Pallas kernels: 48.9 us -> 46 us
  local copies, waits for them, and re-layouts: 1.85 us -> 1.32 us
    pallas_call x1, Pallas kernels: 48.9 us -> 46 us  [on_device(): pl.pallas_call(functools.partial(kernel, owners, slabs, rows), out_shape=...]
    unnamed x6 -> x0, local copies, waits for them, and re-layouts: 1.85 us -> none
    slice x0 -> x1, local copies, waits for them, and re-layouts: none -> 1.32 us  [on_device(): return (result[0:1], result[1:2])]
where the time goes in v3:
time: 48.2 us; the launch traced here: 47.9 us
  Pallas kernels  46 us (95%)
  local copies, waits for them, and re-layouts  1.32 us (3%)
  between operations  0.64 us (1%)
    pallas_call x1, Pallas kernels, on_device(): pl.pallas_call(functools.partial(kernel, owners, slabs, rows), out_shape=...  46 us
    slice x1, local copies, waits for them, and re-layouts, on_device(): return (result[0:1], result[1:2])  1.32 us

profile of v3, /device:TPU:1, one launch (start us, length us, event | category | flops | bytes accessed | tf_op | source)
XLA Modules:
  0.0 47.9 jit_solution(8635296620246544228)
XLA Ops:
  0.6 46.0 %shard_map.68 = f32[2,256]{1,0:T(2,128)} custom-call(f32[2,128,512]{2,1,0:T(8,128)} %bitcast.1, f32[16,512]{1,0:T(8,128)} %medium_ref.1, f32[2,256,256]{2,1,0:T(8,128)} %csm_ref.1, f32[2,256,256]{2,1,0:T(8,128)} %weight_ref.1, s32[1,8192]{1,0:T(1,128)} %cells_ref.1), custom_call_target="tpu_custom_call" | custom-call | tf_op jit(solution)/shard_map/pallas_call | solution.py:298
  46.6 1.3 %fusion = (f32[1,256]{1,0:T(1,128)}, f32[1,256]{1,0:T(1,128)}) fusion(f32[2,256]{1,0:T(2,128)} %shard_map.68), kind=kLoop, calls=%fused_computation | loop fusion | bytes 4096 | tf_op jit(solution)/shard_map/slice | solution.py:328

commit v4 on v3

--- a/solution.py
+++ b/solution.py
@@ -32,6 +32,12 @@
     tiles = cols // LANES
     inner = rows // 2
 
+    def farthest_first(step):
+        odd = lax.rem(step, 2)
+        return lax.rem(
+            me + owners // 2 + odd * (step // 2) + (1 - odd) * (owners - step // 2), owners
+        )
+
     barrier = pltpu.get_barrier_semaphore()
     for other in (above, below):
         pl.semaphore_signal(barrier, inc=1, device_id={"row": other}, device_id_type=MESH)
@@ -140,7 +146,7 @@
     def send_blocks(block):
         @pl.loop(1, owners)
         def _(step):
-            block_copy(block, me, lax.rem(me + step, owners)).start()
+            block_copy(block, me, farthest_first(step)).start()
 
         own = pltpu.make_async_copy(
             outgoing.at[block, me], vectors.at[block, me], local_sem.at[3 + block]
@@ -239,7 +245,7 @@
 
     @pl.loop(1, owners)
     def _(step):
-        result_copy(me, lax.rem(me + step, owners)).start()
+        result_copy(me, farthest_first(step)).start()
 
     own_result = pltpu.make_async_copy(mine, table.at[me], local_sem.at[5])
     own_result.start()

time: 48.2 us -> 47 us (0.975)
  Pallas kernels: 46 us -> 44.6 us
    pallas_call x1, Pallas kernels: 46 us -> 44.6 us  [on_device(): pl.pallas_call(functools.partial(kernel, owners, slabs, rows), out_shape=...]
where the time goes in v4:
time: 47 us; the launch traced here: 46.6 us
  Pallas kernels  44.6 us (95%)
  local copies, waits for them, and re-layouts  1.32 us (3%)
  between operations  0.64 us (1%)
    pallas_call x1, Pallas kernels, on_device(): pl.pallas_call(functools.partial(kernel, owners, slabs, rows), out_shape=...  44.6 us
    slice x1, local copies, waits for them, and re-layouts, on_device(): return (result[0:1], result[1:2])  1.32 us

profile of v4, /device:TPU:1, one launch (start us, length us, event | category | flops | bytes accessed | tf_op | source)
XLA Modules:
  0.0 46.6 jit_solution(13499218380061804794)
XLA Ops:
  0.6 44.6 %shard_map.68 = f32[2,256]{1,0:T(2,128)} custom-call(f32[2,128,512]{2,1,0:T(8,128)} %bitcast.1, f32[16,512]{1,0:T(8,128)} %medium_ref.1, f32[2,256,256]{2,1,0:T(8,128)} %csm_ref.1, f32[2,256,256]{2,1,0:T(8,128)} %weight_ref.1, s32[1,8192]{1,0:T(1,128)} %cells_ref.1), custom_call_target="tpu_custom_call" | custom-call | tf_op jit(solution)/shard_map/pallas_call | solution.py:304
  45.2 1.3 %fusion = (f32[1,256]{1,0:T(1,128)}, f32[1,256]{1,0:T(1,128)}) fusion(f32[2,256]{1,0:T(2,128)} %shard_map.68), kind=kLoop, calls=%fused_computation | loop fusion | bytes 4096 | tf_op jit(solution)/shard_map/slice | solution.py:334

commit v5 on v4

--- a/solution.py
+++ b/solution.py
@@ -205,36 +205,28 @@
     load_weight.wait()
     own_inner.wait()
     own_outer.wait()
+
+    def dot(a, b):
+        return jnp.dot(a, b, precision=lax.Precision.HIGHEST, preferred_element_type=jnp.float32)
+
     for block in range(2):
         @pl.loop(1, owners)
         def _(step):
             block_copy(block, lax.rem(me + step, owners), me).wait_recv()
 
-    def stacked(part):
-        return jnp.concatenate(
-            [vectors[block, :, part].reshape(owners * hydros, LANES) for block in range(2)], axis=1
-        )
-
-    u, v = stacked(0), stacked(1)
-    power = jnp.sum(u * u + v * v, axis=0, keepdims=True) + 1e-06
-
-    def form(matrix):
-        def dot(a, b):
-            return jnp.dot(
-                a, b, precision=lax.Precision.HIGHEST, preferred_element_type=jnp.float32
+        u, v = (vectors[block, :, part].reshape(owners * hydros, LANES) for part in range(2))
+        both = jnp.concatenate([u, v], axis=1)
+
+        def form(matrix):
+            near = dot(matrix[0], both)
+            cross = dot(matrix[1], u)
+            return jnp.sum(
+                u * near[:, :LANES] + v * (near[:, LANES:] + 2.0 * cross), axis=0, keepdims=True
             )
 
-        return jnp.sum(
-            u * dot(matrix[0], u) + v * (dot(matrix[0], v) + 2.0 * dot(matrix[1], u)),
-            axis=0, keepdims=True,
-        )
-
-    bartlett = form(csm) / power
-    capon = power / form(weight)
-    mine[0:1] = bartlett[:, :LANES]
-    mine[1:2] = bartlett[:, LANES:]
-    mine[2:3] = capon[:, :LANES]
-    mine[3:4] = capon[:, LANES:]
+        power = jnp.sum(u * u + v * v, axis=0, keepdims=True) + 1e-06
+        mine[block : block + 1] = form(csm) / power
+        mine[2 + block : 3 + block] = power / form(weight)
 
     def result_copy(source, target):
         return pltpu.make_async_remote_copy(

time: 47 us -> 46.5 us (0.989)
  no operation moved by 1% of the time
where the time goes in v5:
time: 46.5 us; the launch traced here: 46.1 us
  Pallas kernels  44.2 us (95%)
  local copies, waits for them, and re-layouts  1.32 us (3%)
  between operations  0.64 us (1%)
    pallas_call x1, Pallas kernels, on_device(): pl.pallas_call(functools.partial(kernel, owners, slabs, rows), out_shape=...  44.2 us
    slice x1, local copies, waits for them, and re-layouts, on_device(): return (result[0:1], result[1:2])  1.32 us

profile of v5, /device:TPU:1, one launch (start us, length us, event | category | flops | bytes accessed | tf_op | source)
XLA Modules:
  0.0 46.1 jit_solution(12596566884024141603)
XLA Ops:
  0.6 44.2 %shard_map.68 = f32[2,256]{1,0:T(2,128)} custom-call(f32[2,128,512]{2,1,0:T(8,128)} %bitcast.1, f32[16,512]{1,0:T(8,128)} %medium_ref.1, f32[2,256,256]{2,1,0:T(8,128)} %csm_ref.1, f32[2,256,256]{2,1,0:T(8,128)} %weight_ref.1, s32[1,8192]{1,0:T(1,128)} %cells_ref.1), custom_call_target="tpu_custom_call" | custom-call | tf_op jit(solution)/shard_map/pallas_call | solution.py:296
  44.8 1.3 %fusion = (f32[1,256]{1,0:T(1,128)}, f32[1,256]{1,0:T(1,128)}) fusion(f32[2,256]{1,0:T(2,128)} %shard_map.68), kind=kLoop, calls=%fused_computation | loop fusion | bytes 4096 | tf_op jit(solution)/shard_map/slice | solution.py:326
